TPU v7x, 256 devices: a whole 4x4x8 slice. The times are simulated.
256 devices in a mesh: row: 8 (over x, z_hi), col: 8 (over z_lo, core), depth: 4 (over y).
Axes of the slice: x: 4, y: 4, z: 8 (z_hi: 2, z_lo: 4; z = z_hi * 4 + z_lo), core: 2. Of those that a mesh axis runs over, the one named last changes fastest.
Arguments:
- tokens: bfloat16 [1024, 4096], P(('col', 'depth'), 'row'), may hold values from -72 to 72
- norm_gain: float32 [4096], P('row'), may hold values from 0.25 to 1.75
- w_gate: bfloat16 [4096, 14336], P('row', 'col'), may hold values from -0.09375 to 0.09375
- w_up: bfloat16 [4096, 14336], P('row', 'col'), may hold values from -0.09375 to 0.09375
- w_down: bfloat16 [14336, 4096], P('col', 'row'), may hold values from -0.046875 to 0.046875
- cotangent: bfloat16 [1024, 4096], P(('col', 'depth'), 'row'), may hold values from -1.5 to 1.5
Outputs:
- output: bfloat16 [1024, 4096], P(('col', 'depth'), 'row')
- grad_tokens: bfloat16 [1024, 4096], P(('col', 'depth'), 'row')
- grad_gain: float32 [4096], P('row')
- grad_gate: bfloat16 [4096, 14336], P('row', 'col')
- grad_up: bfloat16 [4096, 14336], P('row', 'col')
- grad_down: bfloat16 [14336, 4096], P('col', 'row')
All inputs are finite; a program needn't handle non-finite values.
Results may differ from a plain program's by a relative error of at most 0.023.
Values may be sent and summed in bfloat16 or wider, within the bound.
No kernel may reach another device: no remote copies, remote signals or barrier semaphores. Data moves between devices by JAX's collectives and lax.ppermute only.
A program may use at most 64 MiB of HBM per device.

v0:
```python
import jax
import jax.numpy as jnp
from jax import lax
from jax.sharding import PartitionSpec as P

D = 4096
EPS = 1e-05


def contract_rows(left, right):
    return lax.dot_general(
        left, right, (((0,), (0,)), ((), ())), preferred_element_type=jnp.float32
    )


def contract_cols(left, right):
    return lax.dot_general(
        left, right, (((1,), (1,)), ((), ())), preferred_element_type=jnp.float32
    )


def body(tokens, norm_gain, w_gate, w_up, w_down, cotangent):
    inputs = tokens.astype(jnp.float32)
    sumsq = lax.psum(jnp.sum(inputs * inputs, axis=1), "row")
    inv_rms = lax.rsqrt(sumsq / D + EPS)[:, None]
    normal_rows = inputs * inv_rms
    normed = (normal_rows * norm_gain[None, :]).astype(jnp.bfloat16)
    gathered = lax.all_gather(normed, "col", axis=0, tiled=True)
    piece = gathered
    gate = lax.psum_scatter(
        jnp.dot(piece, w_gate, preferred_element_type=jnp.float32).astype(jnp.bfloat16),
        "row",
        scatter_dimension=0,
        tiled=True,
    ).astype(jnp.float32)
    piece = gathered
    up = lax.psum_scatter(
        jnp.dot(piece, w_up, preferred_element_type=jnp.float32).astype(jnp.bfloat16),
        "row",
        scatter_dimension=0,
        tiled=True,
    ).astype(jnp.float32)
    sig = jax.nn.sigmoid(gate)
    act = gate * sig
    hidden = (act * up).astype(jnp.bfloat16)
    hidden_all = lax.all_gather(hidden, "row", axis=0, tiled=True)
    piece = hidden_all
    mixed = lax.psum_scatter(
        jnp.dot(piece, w_down, preferred_element_type=jnp.float32).astype(jnp.bfloat16),
        "col",
        scatter_dimension=0,
        tiled=True,
    ).astype(jnp.float32)
    output = (inputs + mixed).astype(jnp.bfloat16)
    cot_all = lax.all_gather(cotangent, "col", axis=0, tiled=True)
    piece = cot_all
    grad_hidden = lax.psum_scatter(
        contract_cols(piece, w_down).astype(jnp.bfloat16), "row", scatter_dimension=0, tiled=True
    ).astype(jnp.float32)
    down_grad = contract_rows(hidden_all, cot_all)
    down_sum = lax.psum(down_grad.astype(jnp.bfloat16), "depth")
    grad_up_h = (grad_hidden * act).astype(jnp.bfloat16)
    grad_gate_h = (grad_hidden * up * sig * (1.0 + gate * (1.0 - sig))).astype(jnp.bfloat16)
    gate_all, up_all = (
        lax.all_gather(grad_gate_h, "row", axis=0, tiled=True),
        lax.all_gather(grad_up_h, "row", axis=0, tiled=True),
    )
    gate_grad = contract_rows(gathered, gate_all)
    up_grad = contract_rows(gathered, up_all)
    grad_normed = lax.psum_scatter(
        (contract_cols(gate_all, w_gate) + contract_cols(up_all, w_up)).astype(jnp.bfloat16),
        "col",
        scatter_dimension=0,
        tiled=True,
    ).astype(jnp.float32)
    grad_scaled = grad_normed * norm_gain[None, :]
    proj = lax.psum(jnp.sum(grad_scaled * normal_rows, axis=1), "row")
    grad_tokens = (
        cotangent.astype(jnp.float32) + inv_rms * (grad_scaled - normal_rows * (proj / D)[:, None])
    ).astype(jnp.bfloat16)
    grad_gain = lax.psum(jnp.sum(grad_normed * normal_rows, axis=0), ("col", "depth"))
    gate_sum, up_sum = (
        lax.psum(gate_grad.astype(jnp.bfloat16), "depth").astype(jnp.float32),
        lax.psum(up_grad.astype(jnp.bfloat16), "depth").astype(jnp.float32),
    )
    return (
        output,
        grad_tokens,
        grad_gain,
        gate_sum.astype(jnp.bfloat16),
        up_sum.astype(jnp.bfloat16),
        down_sum,
    )


def solution(mesh):
    in_specs = (
        P(("col", "depth"), "row"),
        P("row"),
        P("row", "col"),
        P("row", "col"),
        P("col", "row"),
        P(("col", "depth"), "row"),
    )
    out_specs = (
        P(("col", "depth"), "row"),
        P(("col", "depth"), "row"),
        P("row"),
        P("row", "col"),
        P("row", "col"),
        P("col", "row"),
    )
    return jax.shard_map(body, mesh=mesh, in_specs=in_specs, out_specs=out_specs, check_vma=False)
```

profile of v0, /device:TPU:1, one launch (start us, length us, event | category | flops | bytes accessed | tf_op | source)
XLA Modules:
  0.0 635.6 jit_solution(9380735947653987925)
XLA Ops:
  7.2 0.0 copy-start
  7.2 0.0 reduce-scatter.12.cloned.1.call-start
  7.2 17.6 %all_gather.17 = bf16[256,512]{1,0:T(8,128)(2,1)S(1)} all-gather(bf16[32,512]{1,0:T(8,128)(2,1)} %param.11), channel_id=1, replica_groups=mesh['row'=8,'col'=8,'depth'=4] {'col'}, dimensions={0}, use_global_device_ids=true | all-gather | bytes 294912 | tf_op jit(solution)/shard_map/all_gather | solution.py:55
  24.8 0.0 copy-start.6
  24.8 0.0 copy-start.8
  24.8 3.1 convolution_convert_fusion.3
  27.9 0.0 reduce-scatter.12.cloned.1.call-update
  27.9 0.0 reduce-scatter.8.cloned.1.call-start
  28.0 0.0 copy-done.6
  28.0 0.1 fusion.21
  28.1 27.7 %psum.42 = f32[32]{0:T(128)S(1)} all-reduce(f32[32]{0:T(128)S(1)} %fusion.21), channel_id=1, replica_groups=mesh['row'=8,'col'=8,'depth'=4] {'row'}, use_global_device_ids=true, to_apply=%region_1.0 | all-reduce | flops 32 | bytes 256 | tf_op jit(solution)/shard_map/psum | solution.py:24
  55.9 0.0 copy-done.8
  55.9 0.1 fusion.18
  56.0 18.4 %all_gather.15 = bf16[256,512]{1,0:T(8,128)(2,1)S(1)} all-gather(bf16[32,512]{1,0:T(8,128)(2,1)S(1)} %fusion.18), channel_id=1, replica_groups=mesh['row'=8,'col'=8,'depth'=4] {'col'}, dimensions={0}, use_global_device_ids=true | all-gather | bytes 294912 | tf_op jit(solution)/shard_map/all_gather | solution.py:28
  74.4 3.1 convolution_convert_fusion.4
  77.5 0.0 reduce-scatter.8.cloned.1.call-update
  77.5 0.0 reduce-scatter.6.cloned.1.call-start
  77.5 0.0 copy-done
  77.5 1.6 convolution_convert_fusion.5
  79.1 0.0 reduce-scatter.6.cloned.1.call-update
  79.1 0.0 reduce-scatter.14.cloned.1.call-start
  79.2 35.7 %reduce-scatter.12.cloned.1.call-done = bf16[32,1792]{1,0:T(8,128)(2,1)} async-done(((bf16[256,1792]{1,0:T(8,128)(2,1)}), bf16[32,1792]{1,0:T(8,128)(2,1)}) %reduce-scatter.12.cloned.1.call-update) | async-done | bytes 114704 | tf_op jit(solution)/shard_map/reduce_scatter | solution.py:57
  114.9 87.8 %reduce-scatter.8.cloned.1.call-done = bf16[32,1792]{1,0:T(8,128)(2,1)} async-done(((bf16[256,1792]{1,0:T(8,128)(2,1)}), bf16[32,1792]{1,0:T(8,128)(2,1)}) %reduce-scatter.8.cloned.1.call-update) | async-done | bytes 114704 | tf_op jit(solution)/shard_map/reduce_scatter | solution.py:37
  202.7 87.7 %reduce-scatter.6.cloned.1.call-done = bf16[32,1792]{1,0:T(8,128)(2,1)} async-done(((bf16[256,1792]{1,0:T(8,128)(2,1)}), bf16[32,1792]{1,0:T(8,128)(2,1)}) %reduce-scatter.6.cloned.1.call-update) | async-done | bytes 114704 | tf_op jit(solution)/shard_map/reduce_scatter | solution.py:30
  290.4 1.1 fusion.5
  291.5 47.7 %all_gather.19 = bf16[256,1792]{1,0:T(8,128)(2,1)S(1)} all-gather(bf16[32,1792]{1,0:T(8,128)(2,1)S(1)} %get-tuple-element.11), channel_id=1, replica_groups=mesh['row'=8,'col'=8,'depth'=4] {'row'}, dimensions={0}, use_global_device_ids=true | all-gather | bytes 1032192 | tf_op jit(solution)/shard_map/all_gather | solution.py:66
  339.2 0.0 copy-start.1
  339.2 48.6 %all_gather.18 = bf16[256,1792]{1,0:T(8,128)(2,1)S(1)} all-gather(bf16[32,1792]{1,0:T(8,128)(2,1)S(1)} %get-tuple-element.12), channel_id=1, replica_groups=mesh['row'=8,'col'=8,'depth'=4] {'row'}, dimensions={0}, use_global_device_ids=true | all-gather | bytes 1032192 | tf_op jit(solution)/shard_map/all_gather | solution.py:65
  387.8 0.0 copy-start.2
  387.8 0.7 fusion.23
  388.5 0.0 copy-done.1
  388.5 0.8 copy-done.2
  389.3 1.4 fusion
  390.7 0.0 reduce-scatter.14.cloned.1.call-update
  390.7 0.0 reduce-scatter.10.cloned.1.call-start
  390.8 46.7 %all_gather.16 = bf16[256,1792]{1,0:T(8,128)(2,1)S(1)} all-gather(bf16[32,1792]{1,0:T(8,128)(2,1)S(1)} %get-tuple-element.13), channel_id=1, replica_groups=mesh['row'=8,'col'=8,'depth'=4] {'row'}, dimensions={0}, use_global_device_ids=true | all-gather | bytes 1032192 | tf_op jit(solution)/shard_map/all_gather | solution.py:46
  437.5 0.0 copy-start.3
  437.5 0.9 copy-done.3
  438.4 2.8 convolution_convert_fusion.6
  441.3 3.1 convolution_convert_fusion
  444.4 0.0 reduce-scatter.10.cloned.1.call-update
  444.4 0.0 all-reduce.3.cloned.1.call-start
  444.4 3.1 convolution_convert_fusion.1
  447.5 1.9 convolution_convert_fusion.2
  449.4 0.0 copy-start.7
  449.4 0.0 all-reduce.3.cloned.1.call-update
  449.5 0.0 reduce-scatter.14.cloned.1.call-done
  449.5 1.0 fusion.20
  450.4 20.6 %psum.43 = f32[32]{0:T(128)S(1)} all-reduce(f32[32]{0:T(128)S(1)} %get-tuple-element.7), channel_id=1, replica_groups=mesh['row'=8,'col'=8,'depth'=4] {'row'}, use_global_device_ids=true, to_apply=%region_8.0 | all-reduce | flops 32 | bytes 256 | tf_op jit(solution)/shard_map/psum | solution.py:77
  471.1 93.6 %psum.44 = f32[512]{0:T(512)} all-reduce(f32[512]{0:T(512)S(1)} %get-tuple-element.6), channel_id=1, replica_groups=mesh['row'=8,'col'=8,'depth'=4] {'col','depth'}, use_global_device_ids=true, to_apply=%region_10.0 | all-reduce | flops 512 | bytes 4096 | tf_op jit(solution)/shard_map/psum | solution.py:81
  564.7 0.0 reduce-scatter.10.cloned.1.call-done
  564.7 0.0 copy-done.7
  564.7 1.5 fusion.17
  566.2 56.2 %all-reduce.3.cloned.1.call-done = (bf16[512,1792]{1,0:T(8,128)(2,1)}, bf16[512,1792]{1,0:T(8,128)(2,1)}, bf16[1792,512]{1,0:T(8,128)(2,1)}) async-done(((bf16[512,1792]{1,0:T(8,128)(2,1)}, bf16[512,1792]{1,0:T(8,128)(2,1)}, bf16[1792,512]{1,0:T(8,128)(2,1)}), (bf16[512,1792]{1,0:T(8,128)(2,1)}, bf16[512,1792]{1,0:T(8,128)(2,1)}, bf16[1792,512]{1,0:T(8,128)(2,1)})) %all-reduce.3.cloned.1.call-update) | async-done | bytes 5505040 | tf_op jit(solution)/shard_map/psum | solution.py:83
  622.4 0.0 copy-start.5
  622.4 3.0 copy.15
  625.4 0.0 copy-done.5
  625.4 0.0 copy-start.4
  625.4 1.2 copy.16
  626.6 0.9 copy-done.4
  627.5 1.2 copy.17
  (2 shorter events, 0.0 us)
Async XLA Ops:
  7.2 70.4 %copy-start = (bf16[512,1792]{1,0:T(8,128)(2,1)S(1)}, bf16[512,1792]{1,0:T(8,128)(2,1)}, u32[]{:S(2)}) copy-start(bf16[512,1792]{1,0:T(8,128)(2,1)} %param.8) | copy-start | bytes 5505028
  7.2 107.7 %reduce-scatter.12.cloned.1.call-start = ((), (), s32[]{:S(2)}) async-start(), calls=%async_computation.8 | async-start | bytes 1032192 | tf_op jit(solution)/shard_map/reduce_scatter | solution.py:57
  24.8 3.2 copy-start.6
  24.8 31.1 %copy-start.8 = (f32[512]{0:T(512)S(1)}, f32[512]{0:T(512)}, u32[]{:S(2)}) copy-start(f32[512]{0:T(512)} %param.7) | copy-start | bytes 6148
  27.9 174.7 %reduce-scatter.8.cloned.1.call-start = ((), (), s32[]{:S(2)}) async-start(), calls=%async_computation.6 | async-start | bytes 1032192 | tf_op jit(solution)/shard_map/reduce_scatter | solution.py:37
  77.5 212.9 %reduce-scatter.6.cloned.1.call-start = ((), (), s32[]{:S(2)}) async-start(), calls=%async_computation.5 | async-start | bytes 1032192 | tf_op jit(solution)/shard_map/reduce_scatter | solution.py:30
  79.1 370.3 %reduce-scatter.14.cloned.1.call-start = ((), (), s32[]{:S(2)}) async-start(), calls=%async_computation.9 | async-start | bytes 294912 | tf_op jit(solution)/shard_map/reduce_scatter | solution.py:70
  339.2 49.3 %copy-start.1 = (bf16[256,1792]{1,0:T(8,128)(2,1)}, bf16[256,1792]{1,0:T(8,128)(2,1)S(1)}, u32[]{:S(2)}) copy-start(bf16[256,1792]{1,0:T(8,128)(2,1)S(1)} %all_gather.19) | copy-start | bytes 2752516
  387.8 1.5 copy-start.2
  390.7 173.9 %reduce-scatter.10.cloned.1.call-start = ((), (), s32[]{:S(2)}) async-start(), calls=%async_computation.7 | async-start | bytes 294912 | tf_op jit(solution)/shard_map/reduce_scatter | solution.py:48
  437.5 0.9 copy-start.3
  444.4 178.0 %all-reduce.3.cloned.1.call-start = ((), (), s32[]{:S(2)}) async-start(), calls=%async_computation.10 | async-start | bytes 11010048 | tf_op jit(solution)/shard_map/psum | solution.py:83
  449.4 115.2 %copy-start.7 = (bf16[32,512]{1,0:T(8,128)(2,1)S(1)}, bf16[32,512]{1,0:T(8,128)(2,1)}, u32[]{:S(2)}) copy-start(bf16[32,512]{1,0:T(8,128)(2,1)} %param.11) | copy-start | bytes 98308
  622.4 3.0 copy-start.5
  625.4 2.2 copy-start.4
Sparse Core Ops, SparseCore 0:
  28.1 86.7 reduce-scatter.11
  119.4 83.2 reduce-scatter.7
  207.2 83.1 reduce-scatter.5
  390.9 47.8 reduce-scatter.13
  444.5 53.3 reduce-scatter.9
  500.8 121.5 all-reduce.2
where the time goes:
time: 636 us
  blocking collectives  321 us (50%)
  waiting for transfers between devices  268 us (42%)
  matrix products  20.7 us (3%)
  between operations  14.2 us (2%)
  local copies, waits for them, and re-layouts  8.14 us (1%)
    psum x1, blocking collectives, body(): lax.psum(jnp.sum(grad_normed * normal_rows, axis=0), ('col', 'depth'))  93.6 us
    reduce_scatter x1, waiting for transfers between devices, body(): lax.psum_scatter(jnp.dot(piece, w_up, preferred_element_type=jnp.float32)...  87.8 us
    reduce_scatter x1, waiting for transfers between devices, body(): lax.psum_scatter(jnp.dot(piece, w_gate, preferred_element_type=jnp.float3...  87.7 us
    psum x1, waiting for transfers between devices, body(): lax.psum(gate_grad.astype(jnp.bfloat16), 'depth').astype(jnp.float32)  56.2 us
    all_gather x1, blocking collectives, body(): lax.all_gather(grad_gate_h, 'row', axis=0, tiled=True)  48.6 us
    all_gather x1, blocking collectives, body(): lax.all_gather(grad_up_h, 'row', axis=0, tiled=True)  47.7 us
    all_gather x1, blocking collectives, body(): hidden_all = lax.all_gather(hidden, 'row', axis=0, tiled=True)  46.7 us
    reduce_scatter x1, waiting for transfers between devices, body(): lax.psum_scatter(contract_cols(piece, w_down).astype(jnp.bfloat16), 'row'...  35.7 us
  transfers between devices with their start and end apart: 6, of which 4 were waited for; matrix products, arithmetic and copies ran while one was open for 3% of the time, Pallas kernels for 0%

commit v1 on v0

--- a/solution.py
+++ b/solution.py
@@ -80,7 +80,9 @@
     ).astype(jnp.bfloat16)
     grad_gain = lax.psum(jnp.sum(grad_normed * normal_rows, axis=0), ("col", "depth"))
     gate_sum, up_sum = (
-        lax.psum(gate_grad.astype(jnp.bfloat16), "depth").astype(jnp.float32),
+        jnp.sum(lax.all_gather(gate_grad.astype(jnp.bfloat16), "depth"), axis=0).astype(
+            jnp.float32
+        ),
         lax.psum(up_grad.astype(jnp.bfloat16), "depth").astype(jnp.float32),
     )
     return (

time: 636 us -> 681 us (1.071)
  waiting for transfers between devices: 268 us -> 309 us
    psum x1, waiting for transfers between devices: 56.2 us -> 86.8 us  [body(): lax.psum(up_grad.astype(jnp.bfloat16), 'depth').astype(jnp.float32)]
    all_gather x0 -> x1, waiting for transfers between devices: none -> 10.8 us  [body(): lax.all_gather(gate_grad.astype(jnp.bfloat16), 'depth')]
  transfers between devices with their start and end apart: 6 -> 7, of which waited for: 4 -> 5; matrix products, arithmetic and copies ran while one was open for 3% -> 3% of each run, Pallas kernels for 0% -> 0%
where the time goes in v1:
time: 681 us
  blocking collectives  323 us (47%)
  waiting for transfers between devices  309 us (45%)
  matrix products  19.6 us (3%)
  between operations  14.2 us (2%)
  other arithmetic  9.68 us (1%)
    psum x1, blocking collectives, body(): lax.psum(jnp.sum(grad_normed * normal_rows, axis=0), ('col', 'depth'))  93.3 us
    reduce_scatter x1, waiting for transfers between devices, body(): lax.psum_scatter(jnp.dot(piece, w_up, preferred_element_type=jnp.float32)...  87.9 us
    reduce_scatter x1, waiting for transfers between devices, body(): lax.psum_scatter(jnp.dot(piece, w_gate, preferred_element_type=jnp.float3...  87.8 us
    psum x1, waiting for transfers between devices, body(): lax.psum(up_grad.astype(jnp.bfloat16), 'depth').astype(jnp.float32)  86.8 us
    all_gather x1, blocking collectives, body(): lax.all_gather(grad_gate_h, 'row', axis=0, tiled=True)  47.8 us
    all_gather x1, blocking collectives, body(): hidden_all = lax.all_gather(hidden, 'row', axis=0, tiled=True)  47.3 us
    all_gather x1, blocking collectives, body(): lax.all_gather(grad_up_h, 'row', axis=0, tiled=True)  47.2 us
    reduce_scatter x1, waiting for transfers between devices, body(): lax.psum_scatter(contract_cols(piece, w_down).astype(jnp.bfloat16), 'row'...  35.7 us
  transfers between devices with their start and end apart: 7, of which 5 were waited for; matrix products, arithmetic and copies ran while one was open for 3% of the time, Pallas kernels for 0%

profile of v1, /device:TPU:1, one launch (start us, length us, event | category | flops | bytes accessed | tf_op | source)
XLA Modules:
  0.0 681.0 jit_solution(5942030839492682610)
XLA Ops:
  7.2 0.0 copy-start
  7.2 0.0 reduce-scatter.12.cloned.1.call-start
  7.2 17.6 %all_gather.23 = bf16[256,512]{1,0:T(8,128)(2,1)S(1)} all-gather(bf16[32,512]{1,0:T(8,128)(2,1)} %param.11), channel_id=1, replica_groups=mesh['row'=8,'col'=8,'depth'=4] {'col'}, dimensions={0}, use_global_device_ids=true | all-gather | bytes 294912 | tf_op jit(solution)/shard_map/all_gather | solution.py:55
  24.8 0.0 copy-start.6
  24.8 0.0 copy-start.8
  24.8 3.1 convolution_convert_fusion.3
  27.9 0.0 reduce-scatter.12.cloned.1.call-update
  27.9 0.0 reduce-scatter.6.cloned.1.call-start
  28.0 0.0 copy-done.6
  28.0 0.1 fusion.21
  28.1 27.7 %psum.35 = f32[32]{0:T(128)S(1)} all-reduce(f32[32]{0:T(128)S(1)} %fusion.21), channel_id=1, replica_groups=mesh['row'=8,'col'=8,'depth'=4] {'row'}, use_global_device_ids=true, to_apply=%region_1.0 | all-reduce | flops 32 | bytes 256 | tf_op jit(solution)/shard_map/psum | solution.py:24
  55.9 0.0 copy-done.8
  55.9 0.1 fusion.18
  56.0 18.4 %all_gather.21 = bf16[256,512]{1,0:T(8,128)(2,1)S(1)} all-gather(bf16[32,512]{1,0:T(8,128)(2,1)S(1)} %fusion.18), channel_id=1, replica_groups=mesh['row'=8,'col'=8,'depth'=4] {'col'}, dimensions={0}, use_global_device_ids=true | all-gather | bytes 294912 | tf_op jit(solution)/shard_map/all_gather | solution.py:28
  74.4 0.0 copy-done
  74.4 1.6 convolution_convert_fusion.5
  76.0 0.0 reduce-scatter.6.cloned.1.call-update
  76.0 0.0 reduce-scatter.8.cloned.1.call-start
  76.0 3.1 convolution_convert_fusion.4
  79.1 0.0 reduce-scatter.8.cloned.1.call-update
  79.1 0.0 reduce-scatter.14.cloned.1.call-start
  79.2 35.7 %reduce-scatter.12.cloned.1.call-done = bf16[32,1792]{1,0:T(8,128)(2,1)} async-done(((bf16[256,1792]{1,0:T(8,128)(2,1)}), bf16[32,1792]{1,0:T(8,128)(2,1)}) %reduce-scatter.12.cloned.1.call-update) | async-done | bytes 114704 | tf_op jit(solution)/shard_map/reduce_scatter | solution.py:57
  114.9 87.8 %reduce-scatter.6.cloned.1.call-done = bf16[32,1792]{1,0:T(8,128)(2,1)} async-done(((bf16[256,1792]{1,0:T(8,128)(2,1)}), bf16[32,1792]{1,0:T(8,128)(2,1)}) %reduce-scatter.6.cloned.1.call-update) | async-done | bytes 114704 | tf_op jit(solution)/shard_map/reduce_scatter | solution.py:30
  202.7 87.9 %reduce-scatter.8.cloned.1.call-done = bf16[32,1792]{1,0:T(8,128)(2,1)} async-done(((bf16[256,1792]{1,0:T(8,128)(2,1)}), bf16[32,1792]{1,0:T(8,128)(2,1)}) %reduce-scatter.8.cloned.1.call-update) | async-done | bytes 114704 | tf_op jit(solution)/shard_map/reduce_scatter | solution.py:37
  290.5 1.1 fusion.5
  291.7 47.8 %all_gather.24 = bf16[256,1792]{1,0:T(8,128)(2,1)S(1)} all-gather(bf16[32,1792]{1,0:T(8,128)(2,1)S(1)} %get-tuple-element.11), channel_id=1, replica_groups=mesh['row'=8,'col'=8,'depth'=4] {'row'}, dimensions={0}, use_global_device_ids=true | all-gather | bytes 1032192 | tf_op jit(solution)/shard_map/all_gather | solution.py:65
  339.4 0.0 copy-start.1
  339.4 0.0 copy-start.2
  339.4 0.7 fusion.23
  340.1 0.2 copy-done.1
  340.4 47.2 %all_gather.25 = bf16[256,1792]{1,0:T(8,128)(2,1)S(1)} all-gather(bf16[32,1792]{1,0:T(8,128)(2,1)S(1)} %get-tuple-element.10), channel_id=1, replica_groups=mesh['row'=8,'col'=8,'depth'=4] {'row'}, dimensions={0}, use_global_device_ids=true | all-gather | bytes 1032192 | tf_op jit(solution)/shard_map/all_gather | solution.py:66
  387.6 0.0 copy-done.2
  387.6 1.4 fusion
  389.0 0.0 reduce-scatter.14.cloned.1.call-update
  389.0 0.0 reduce-scatter.10.cloned.1.call-start
  389.0 47.3 %all_gather.22 = bf16[256,1792]{1,0:T(8,128)(2,1)S(1)} all-gather(bf16[32,1792]{1,0:T(8,128)(2,1)S(1)} %get-tuple-element.12), channel_id=1, replica_groups=mesh['row'=8,'col'=8,'depth'=4] {'row'}, dimensions={0}, use_global_device_ids=true | all-gather | bytes 1032192 | tf_op jit(solution)/shard_map/all_gather | solution.py:46
  436.4 0.0 copy-start.3
  436.4 0.9 copy-done.3
  437.3 2.9 convolution_convert_fusion.6
  440.2 0.0 reduce-scatter.10.cloned.1.call-update
  440.2 0.0 all-gather.3.cloned.1.call-start
  440.2 3.1 convolution_convert_fusion.2
  443.3 0.0 all-gather.3.cloned.1.call-update
  443.3 0.0 all-reduce.3.cloned.1.call-start
  443.4 0.0 copy-start.4
  443.4 1.9 convolution_convert_fusion.1
  445.3 0.0 copy-done.4
  445.3 1.9 convolution_convert_fusion
  447.2 0.0 copy-start.7
  447.2 0.0 all-reduce.3.cloned.1.call-update
  447.3 0.0 reduce-scatter.14.cloned.1.call-done
  447.3 1.0 fusion.20
  448.2 23.4 %psum.36 = f32[32]{0:T(128)S(1)} all-reduce(f32[32]{0:T(128)S(1)} %get-tuple-element.7), channel_id=1, replica_groups=mesh['row'=8,'col'=8,'depth'=4] {'row'}, use_global_device_ids=true, to_apply=%region_8.0 | all-reduce | flops 32 | bytes 256 | tf_op jit(solution)/shard_map/psum | solution.py:77
  471.6 93.3 %psum.37 = f32[512]{0:T(512)} all-reduce(f32[512]{0:T(512)S(1)} %get-tuple-element.6), channel_id=1, replica_groups=mesh['row'=8,'col'=8,'depth'=4] {'col','depth'}, use_global_device_ids=true, to_apply=%region_10.0 | all-reduce | flops 512 | bytes 4096 | tf_op jit(solution)/shard_map/psum | solution.py:81
  564.9 0.0 reduce-scatter.10.cloned.1.call-done
  564.9 0.0 copy-done.7
  564.9 1.5 fusion.17
  566.4 10.8 %all-gather.3.cloned.1.call-done = bf16[2048,1792]{1,0:T(8,128)(2,1)} async-done(((bf16[512,1792]{1,0:T(8,128)(2,1)}), bf16[2048,1792]{1,0:T(8,128)(2,1)}) %all-gather.3.cloned.1.call-update) | async-done | bytes 7340048 | tf_op jit(solution)/shard_map/all_gather | solution.py:83
  577.2 5.9 reduce_sum.42
  583.1 86.8 %all-reduce.3.cloned.1.call-done = (bf16[512,1792]{1,0:T(8,128)(2,1)}, bf16[1792,512]{1,0:T(8,128)(2,1)}) async-done(((bf16[512,1792]{1,0:T(8,128)(2,1)}, bf16[1792,512]{1,0:T(8,128)(2,1)}), (bf16[512,1792]{1,0:T(8,128)(2,1)}, bf16[1792,512]{1,0:T(8,128)(2,1)})) %all-reduce.3.cloned.1.call-update) | async-done | bytes 3670032 | tf_op jit(solution)/shard_map/psum | solution.py:86
  669.9 0.0 copy-start.5
  669.9 3.0 copy.14
  672.9 0.0 copy-done.5
  672.9 1.2 copy.15
  (2 shorter events, 0.0 us)
Async XLA Ops:
  7.2 67.2 %copy-start = (bf16[512,1792]{1,0:T(8,128)(2,1)S(1)}, bf16[512,1792]{1,0:T(8,128)(2,1)}, u32[]{:S(2)}) copy-start(bf16[512,1792]{1,0:T(8,128)(2,1)} %param.8) | copy-start | bytes 5505028
  7.2 107.7 %reduce-scatter.12.cloned.1.call-start = ((), (), s32[]{:S(2)}) async-start(), calls=%async_computation.8 | async-start | bytes 1032192 | tf_op jit(solution)/shard_map/reduce_scatter | solution.py:57
  24.8 3.2 copy-start.6
  24.8 31.1 %copy-start.8 = (f32[512]{0:T(512)S(1)}, f32[512]{0:T(512)}, u32[]{:S(2)}) copy-start(f32[512]{0:T(512)} %param.7) | copy-start | bytes 6148
  27.9 174.7 %reduce-scatter.6.cloned.1.call-start = ((), (), s32[]{:S(2)}) async-start(), calls=%async_computation.5 | async-start | bytes 1032192 | tf_op jit(solution)/shard_map/reduce_scatter | solution.py:30
  76.0 214.5 %reduce-scatter.8.cloned.1.call-start = ((), (), s32[]{:S(2)}) async-start(), calls=%async_computation.6 | async-start | bytes 1032192 | tf_op jit(solution)/shard_map/reduce_scatter | solution.py:37
  79.1 368.1 %reduce-scatter.14.cloned.1.call-start = ((), (), s32[]{:S(2)}) async-start(), calls=%async_computation.9 | async-start | bytes 294912 | tf_op jit(solution)/shard_map/reduce_scatter | solution.py:70
  339.4 0.9 copy-start.1
  339.4 48.1 %copy-start.2 = (bf16[512,1792]{1,0:T(8,128)(2,1)S(1)}, bf16[512,1792]{1,0:T(8,128)(2,1)}, u32[]{:S(2)}) copy-start(bf16[512,1792]{1,0:T(8,128)(2,1)} %param.9) | copy-start | bytes 5505028
  389.0 176.0 %reduce-scatter.10.cloned.1.call-start = ((), (), s32[]{:S(2)}) async-start(), calls=%async_computation.7 | async-start | bytes 294912 | tf_op jit(solution)/shard_map/reduce_scatter | solution.py:48
  436.4 0.9 copy-start.3
  440.2 137.0 %all-gather.3.cloned.1.call-start = ((), (), s32[]{:S(2)}) async-start(), calls=%async_computation.10 | async-start | bytes 9175040 | tf_op jit(solution)/shard_map/all_gather | solution.py:83
  443.3 226.6 %all-reduce.3.cloned.1.call-start = ((), (), s32[]{:S(2)}) async-start(), calls=%async_computation.11 | async-start | bytes 7340032 | tf_op jit(solution)/shard_map/psum | solution.py:86
  443.4 1.9 copy-start.4
  447.2 117.7 %copy-start.7 = (bf16[32,512]{1,0:T(8,128)(2,1)S(1)}, bf16[32,512]{1,0:T(8,128)(2,1)}, u32[]{:S(2)}) copy-start(bf16[32,512]{1,0:T(8,128)(2,1)} %param.11) | copy-start | bytes 98308
  669.9 3.0 copy-start.5
Sparse Core Ops, SparseCore 0:
  28.1 86.7 reduce-scatter.11
  119.4 83.2 reduce-scatter.5
  207.2 83.2 reduce-scatter.7
  389.1 48.8 reduce-scatter.13
  440.3 55.2 reduce-scatter.9
  497.9 79.2 all-gather.2
  580.1 89.7 all-reduce.2
